TPU v7x, 32 devices: a whole 2x2x4 slice. The times are simulated.
32 devices in a mesh: fsdp: 8 (over y, x, core), tp: 4 (over z).
Axes of the slice: x: 2, y: 2, z: 4, core: 2. Of those that a mesh axis runs over, the one named last changes fastest.
Arguments:
- tokens: bfloat16 [8192, 2048], P(('fsdp', 'tp')), may hold values from -6 to 6
- norm1_gain: float32 [2048], replicated, may hold values from 0.25 to 1.75
- norm1_shift: float32 [2048], replicated, may hold values from -1 to 1
- w_query: bfloat16 [2048, 2048], P('fsdp', 'tp'), may hold values from -0.125 to 0.125
- b_query: float32 [2048], P('tp'), may hold values from -1 to 1
- w_key: bfloat16 [2048, 2048], P('fsdp', 'tp'), may hold values from -0.125 to 0.125
- w_value: bfloat16 [2048, 2048], P('fsdp', 'tp'), may hold values from -0.125 to 0.125
- b_value: float32 [2048], P('tp'), may hold values from -1 to 1
- w_out: bfloat16 [2048, 2048], P('fsdp', 'tp'), may hold values from -0.5 to 0.5
- b_out: float32 [2048], replicated, may hold values from -1 to 1
- norm2_gain: float32 [2048], replicated, may hold values from 0.25 to 1.75
- norm2_shift: float32 [2048], replicated, may hold values from -1 to 1
- w_up: bfloat16 [2048, 8192], P('fsdp', 'tp'), may hold values from -0.125 to 0.125
- b_up: float32 [8192], P('tp'), may hold values from -1 to 1
- w_down: bfloat16 [2048, 8192], P('fsdp', 'tp'), may hold values from -0.09375 to 0.09375
- b_down: float32 [2048], replicated, may hold values from -1 to 1
- teacher: bfloat16 [8192, 2048], P(('fsdp', 'tp')), may hold values from -6 to 6
- valid_mask: int32 [8192], P(('fsdp', 'tp')), may hold values from 0 to 1, as said below
- parents: int32 [8, 8], P('fsdp'), may hold values from -1 to 6, as said below
- summary: int32 [8, 8, 12], P('fsdp'), may hold values from 0 to 127, as said below
Outputs:
- output_states: bfloat16 [8192, 2048], P(('fsdp', 'tp'))
- mean_loss: float32 [], replicated
- grad_tokens: float32 [8192, 2048], P(('fsdp', 'tp'))
- grad_norm1_gain: float32 [2048], replicated
- grad_norm1_shift: float32 [2048], replicated
- grad_w_query: float32 [2048, 2048], P('fsdp', 'tp')
- grad_b_query: float32 [2048], P('tp')
- grad_w_key: float32 [2048, 2048], P('fsdp', 'tp')
- grad_w_value: float32 [2048, 2048], P('fsdp', 'tp')
- grad_b_value: float32 [2048], P('tp')
- grad_w_out: float32 [2048, 2048], P('fsdp', 'tp')
- grad_b_out: float32 [2048], replicated
- grad_norm2_gain: float32 [2048], replicated
- grad_norm2_shift: float32 [2048], replicated
- grad_w_up: float32 [2048, 8192], P('fsdp', 'tp')
- grad_b_up: float32 [8192], P('tp')
- grad_w_down: float32 [2048, 8192], P('fsdp', 'tp')
- grad_b_down: float32 [2048], replicated
Inputs may be any that keep to these rules, and one draw needn't show every extreme that they name: valid_mask is 1 at the first token of every tree. parents[f, 0] is -1 and 0 <= parents[f, s] < s for every later segment s; the last segment of every tree has the segment before it as parent. `summary`: the 12 offsets of one segment are distinct.
All inputs are finite; a program needn't handle non-finite values.
Results may differ from a plain program's by a relative error of at most 0.019.
Values may be sent and summed in bfloat16 or wider, within the bound.
No kernel may reach another device: no remote copies, remote signals or barrier semaphores. Data moves between devices by JAX's collectives and lax.ppermute only.
A program may use at most 192 MiB of HBM per device.

v0:
```python
import jax
import jax.numpy as jnp
from jax import lax
from jax.sharding import PartitionSpec as P

HD = 64
EPSILON = 1e-05
MASKED_SCORE = -1e30


def layer_norm(vectors, norm_gain, norm_shift):
    centre = jnp.mean(vectors, axis=-1, keepdims=True)
    centred = vectors - centre
    spread = jnp.mean(centred * centred, axis=-1, keepdims=True)
    return centred * lax.rsqrt(spread + EPSILON) * norm_gain + norm_shift


def ancestors(parent_row):
    segments = parent_row.shape[0]
    columns = jnp.arange(segments, dtype=jnp.int32)

    def follow(sweep, state_pair):
        ancestry, current = state_pair
        matches = current[:, None] == columns[None, :]
        ancestry = jnp.maximum(ancestry, matches.astype(jnp.float32))
        following = jnp.sum(jnp.where(matches, parent_row[None, :], 0), axis=1)
        current = jnp.where(current >= 0, following, -1)
        return (ancestry, current)

    start_table = jnp.zeros((segments, segments), jnp.float32)
    ancestry, finished = lax.fori_loop(0, segments, follow, (start_table, parent_row))
    return ancestry


def tree_tables(parent_row, summary_rows, length):
    segments = parent_row.shape[0]
    seg_length = length // segments
    ancestry = ancestors(parent_row)
    offsets = jnp.arange(seg_length, dtype=jnp.int32)
    marked = jnp.max(
        (summary_rows[:, :, None] == offsets[None, None, :]).astype(jnp.float32), axis=1
    ).reshape(length)
    key_segment = jnp.arange(length, dtype=jnp.int32) // seg_length
    key_onehot = (key_segment[:, None] == jnp.arange(segments, dtype=jnp.int32)[None, :]).astype(
        jnp.float32
    )
    return (ancestry, marked, key_segment, key_onehot, seg_length)


def block_mask(tables, start_row, block_rows):
    ancestry, marked, key_segment, key_onehot, seg_length = tables
    query_position = start_row + jnp.arange(block_rows, dtype=jnp.int32)
    query_segment = query_position // seg_length
    query_onehot = (
        query_segment[:, None] == jnp.arange(ancestry.shape[0], dtype=jnp.int32)[None, :]
    ).astype(jnp.float32)
    reached = jnp.dot(jnp.dot(query_onehot, ancestry, precision=None), key_onehot.T, precision=None)
    key_position = jnp.arange(marked.shape[0], dtype=jnp.int32)
    same_segment = (query_segment[:, None] == key_segment[None, :]) & (
        key_position[None, :] <= query_position[:, None]
    )
    return same_segment | (reached > 0.5) & (marked[None, :] > 0.5)


def contract(left_side, right_side, left_dim, right_dim):
    return lax.dot_general(
        left_side,
        right_side,
        (((left_dim,), (right_dim,)), ((), ())),
        preferred_element_type=jnp.float32,
    )


def attend_forward(queries, key_states, value_states, tables):
    length = queries.shape[0]
    head_count = queries.shape[1] // HD
    block_rows = min(512, length)
    query_heads = queries.reshape(length, head_count, HD)
    key_heads = key_states.reshape(length, head_count, HD)
    value_heads = value_states.reshape(length, head_count, HD)

    def one_block(start_row):
        query_block = lax.dynamic_slice_in_dim(query_heads, start_row, block_rows, 0)
        scores = jnp.einsum(
            "qhd,khd->hqk", query_block, key_heads, preferred_element_type=jnp.float32
        )
        allowed = block_mask(tables, start_row, block_rows)
        scores = jnp.where(allowed[None], scores, MASKED_SCORE)
        highest = jnp.max(scores, axis=-1, keepdims=True)
        exp_scores = jnp.exp(scores - highest)
        totals = jnp.sum(exp_scores, axis=-1, keepdims=True)
        shares = (exp_scores / totals).astype(jnp.bfloat16)
        attended = jnp.einsum(
            "hqk,khd->qhd", shares, value_heads, preferred_element_type=jnp.float32
        )
        return (attended.astype(jnp.bfloat16), (highest + jnp.log(totals))[..., 0])

    starts = jnp.arange(length // block_rows, dtype=jnp.int32) * block_rows
    attended, log_totals = lax.map(one_block, starts)
    return (attended.reshape(length, head_count * HD), log_totals)


def attend_backward(queries, key_states, value_states, grad_attended, log_totals, tables):
    length = queries.shape[0]
    head_count = queries.shape[1] // HD
    block_rows = min(512, length)
    query_heads = queries.reshape(length, head_count, HD)
    key_heads = key_states.reshape(length, head_count, HD)
    value_heads = value_states.reshape(length, head_count, HD)
    grad_heads = grad_attended.reshape(length, head_count, HD)

    def one_block(summed, members):
        start_row, log_block = members
        key_sum, value_sum = summed
        query_block = lax.dynamic_slice_in_dim(query_heads, start_row, block_rows, 0)
        grad_block = lax.dynamic_slice_in_dim(grad_heads, start_row, block_rows, 0)
        scores = jnp.einsum(
            "qhd,khd->hqk", query_block, key_heads, preferred_element_type=jnp.float32
        )
        allowed = block_mask(tables, start_row, block_rows)
        probs = jnp.where(allowed[None], jnp.exp(scores - log_block[..., None]), 0.0)
        grad_probs = jnp.einsum(
            "qhd,khd->hqk", grad_block, value_heads, preferred_element_type=jnp.float32
        )
        inner_sum = jnp.sum(probs * grad_probs, axis=-1, keepdims=True)
        grad_scores = (probs * (grad_probs - inner_sum)).astype(jnp.bfloat16)
        grad_query = jnp.einsum(
            "hqk,khd->qhd", grad_scores, key_heads, preferred_element_type=jnp.float32
        ).astype(jnp.bfloat16)
        key_sum = key_sum + jnp.einsum(
            "hqk,qhd->khd", grad_scores, query_block, preferred_element_type=jnp.float32
        )
        value_sum = value_sum + jnp.einsum(
            "hqk,qhd->khd",
            probs.astype(jnp.bfloat16),
            grad_block,
            preferred_element_type=jnp.float32,
        )
        return ((key_sum, value_sum), grad_query)

    starts = jnp.arange(length // block_rows, dtype=jnp.int32) * block_rows
    zero_heads = jnp.zeros((length, head_count, HD), jnp.float32)
    (key_sum, value_sum), grad_queries = lax.scan(
        one_block, (zero_heads, zero_heads), (starts, log_totals)
    )
    width = head_count * HD
    return (
        grad_queries.reshape(length, width),
        key_sum.reshape(length, width).astype(jnp.bfloat16),
        value_sum.reshape(length, width).astype(jnp.bfloat16),
    )


def scatter_narrow(partial_sums, axis):
    narrow_sums = lax.psum_scatter(
        partial_sums.astype(jnp.bfloat16), axis, scatter_dimension=0, tiled=True
    )
    return narrow_sums.astype(jnp.float32)


def body(
    tokens,
    norm1_gain,
    norm1_shift,
    w_query,
    b_query,
    w_key,
    w_value,
    b_value,
    w_out,
    b_out,
    norm2_gain,
    norm2_shift,
    w_up,
    b_up,
    w_down,
    b_down,
    teacher,
    valid_mask,
    parents,
    summary,
):

    def attention_weights():
        return (
            lax.all_gather(w_query, "fsdp", axis=0, tiled=True),
            lax.all_gather(w_key, "fsdp", axis=0, tiled=True),
            lax.all_gather(w_value, "fsdp", axis=0, tiled=True),
            lax.all_gather(w_out, "fsdp", axis=0, tiled=True),
        )

    def feed_weights():
        return (
            lax.all_gather(w_up, "fsdp", axis=0, tiled=True),
            lax.all_gather(w_down, "fsdp", axis=0, tiled=True),
        )

    inputs = tokens.astype(jnp.float32)
    normed = layer_norm(inputs, norm1_gain, norm1_shift).astype(jnp.bfloat16)
    normed_all = lax.all_gather(normed, "tp", axis=0, tiled=True)
    full_query, full_key, full_value, full_out = attention_weights()
    queries = (
        (jnp.dot(normed_all, full_query, preferred_element_type=jnp.float32) + b_query) * 0.125
    ).astype(jnp.bfloat16)
    key_states = jnp.dot(normed_all, full_key, preferred_element_type=jnp.float32).astype(
        jnp.bfloat16
    )
    value_states = (
        jnp.dot(normed_all, full_value, preferred_element_type=jnp.float32) + b_value
    ).astype(jnp.bfloat16)
    tables = tree_tables(parents[0], summary[0], normed_all.shape[0])
    attended, log_totals = attend_forward(queries, key_states, value_states, tables)
    branch = scatter_narrow(contract(attended, full_out, 1, 1), "tp")
    hidden = inputs + branch + b_out
    normed_mid = layer_norm(hidden, norm2_gain, norm2_shift).astype(jnp.bfloat16)
    normed_mid_all = lax.all_gather(normed_mid, "tp", axis=0, tiled=True)
    full_up, full_down = feed_weights()
    active = jnp.maximum(
        jnp.dot(normed_mid_all, full_up, preferred_element_type=jnp.float32) + b_up, 0.0
    ).astype(jnp.bfloat16)
    feed_out = scatter_narrow(contract(active, full_down, 1, 1), "tp")
    output = hidden + feed_out + b_down
    weight_mask = valid_mask.astype(jnp.float32)
    deviation = output - teacher.astype(jnp.float32)
    valid_count, squares = lax.psum(
        (jnp.sum(weight_mask), jnp.sum(weight_mask[:, None] * deviation * deviation)),
        ("fsdp", "tp"),
    )
    mean_loss = squares / (valid_count * tokens.shape[1])
    total_tokens = tokens.shape[0] * lax.axis_size("fsdp") * lax.axis_size("tp")
    grad_output = 2.0 * total_tokens / valid_count * weight_mask[:, None] * deviation
    grad_feed_all = lax.all_gather(grad_output.astype(jnp.bfloat16), "tp", axis=0, tiled=True)
    full_up, full_down = feed_weights()
    grad_w_down = contract(grad_feed_all, active, 0, 0)
    grad_pre = jnp.where(
        active > 0, jnp.dot(grad_feed_all, full_down, preferred_element_type=jnp.float32), 0.0
    ).astype(jnp.bfloat16)
    grad_w_up = contract(normed_mid_all, grad_pre, 0, 0)
    grad_w_up, grad_w_down = (
        lax.psum_scatter(
            grad_w_up.astype(jnp.bfloat16), "fsdp", scatter_dimension=0, tiled=True
        ).astype(jnp.float32),
        lax.psum_scatter(
            grad_w_down.astype(jnp.bfloat16), "fsdp", scatter_dimension=0, tiled=True
        ).astype(jnp.float32),
    )
    grad_mid = scatter_narrow(contract(grad_pre, full_up, 1, 1), "tp")
    second_norm, second_pull = jax.vjp(layer_norm, hidden, norm2_gain, norm2_shift)
    grad_hidden_norm, grad_norm2_gain, grad_norm2_shift = second_pull(grad_mid)
    grad_hidden = grad_output + grad_hidden_norm
    grad_branch_all = lax.all_gather(grad_hidden.astype(jnp.bfloat16), "tp", axis=0, tiled=True)
    full_query, full_key, full_value, full_out = attention_weights()
    grad_w_out = contract(grad_branch_all, attended, 0, 0)
    grad_attended = jnp.dot(grad_branch_all, full_out, preferred_element_type=jnp.float32).astype(
        jnp.bfloat16
    )
    grad_queries, grad_keys, grad_values = attend_backward(
        queries, key_states, value_states, grad_attended, log_totals, tables
    )
    grad_pre_query = grad_queries * jnp.bfloat16(0.125)
    grad_w_query = contract(normed_all, grad_pre_query, 0, 0)
    grad_w_key = contract(normed_all, grad_keys, 0, 0)
    grad_w_value = contract(normed_all, grad_values, 0, 0)
    grad_w_query, grad_w_key, grad_w_value, grad_w_out = (
        scatter_narrow(grad_w_query, "fsdp"),
        scatter_narrow(grad_w_key, "fsdp"),
        scatter_narrow(grad_w_value, "fsdp"),
        scatter_narrow(grad_w_out, "fsdp"),
    )
    grad_normed = (
        contract(grad_pre_query, full_query, 1, 1)
        + contract(grad_keys, full_key, 1, 1)
        + contract(grad_values, full_value, 1, 1)
    )
    grad_normed = scatter_narrow(grad_normed, "tp")
    first_norm, first_pull = jax.vjp(layer_norm, inputs, norm1_gain, norm1_shift)
    grad_input_norm, grad_norm1_gain, grad_norm1_shift = first_pull(grad_normed)
    grad_tokens = grad_hidden + grad_input_norm
    column = lax.axis_index("tp")
    tp_count = lax.axis_size("tp")

    def widen(share_part):
        widened = jnp.zeros((share_part.shape[0] * tp_count,), jnp.float32)
        return lax.dynamic_update_slice_in_dim(widened, share_part, column * share_part.shape[0], 0)

    def narrow(widened, span_width):
        return lax.dynamic_slice_in_dim(widened, column * span_width, span_width, 0)

    summed = lax.psum(
        (
            grad_norm1_gain,
            grad_norm1_shift,
            widen(jnp.sum(grad_pre_query.astype(jnp.float32), axis=0)),
            widen(jnp.sum(grad_values.astype(jnp.float32), axis=0)),
            jnp.sum(grad_hidden, axis=0),
            grad_norm2_gain,
            grad_norm2_shift,
            widen(jnp.sum(grad_pre.astype(jnp.float32), axis=0)),
            jnp.sum(grad_output, axis=0),
        ),
        ("fsdp", "tp"),
    )
    return (
        output.astype(jnp.bfloat16),
        mean_loss,
        grad_tokens,
        summed[0],
        summed[1],
        grad_w_query,
        narrow(summed[2], b_query.shape[0]),
        grad_w_key,
        grad_w_value,
        narrow(summed[3], b_value.shape[0]),
        grad_w_out,
        summed[4],
        summed[5],
        summed[6],
        grad_w_up,
        narrow(summed[7], b_up.shape[0]),
        grad_w_down,
        summed[8],
    )


def solution(mesh):
    placed = (
        P(("fsdp", "tp"), None),
        P(),
        P(),
        P("fsdp", "tp"),
        P("tp"),
        P("fsdp", "tp"),
        P("fsdp", "tp"),
        P("tp"),
        P("fsdp", "tp"),
        P(),
        P(),
        P(),
        P("fsdp", "tp"),
        P("tp"),
        P("fsdp", "tp"),
        P(),
        P(("fsdp", "tp"), None),
        P(("fsdp", "tp")),
        P("fsdp", None),
        P("fsdp", None, None),
    )
    return jax.shard_map(
        body,
        mesh=mesh,
        in_specs=placed,
        out_specs=(
            P(("fsdp", "tp"), None),
            P(),
            P(("fsdp", "tp"), None),
            P(),
            P(),
            P("fsdp", "tp"),
            P("tp"),
            P("fsdp", "tp"),
            P("fsdp", "tp"),
            P("tp"),
            P("fsdp", "tp"),
            P(),
            P(),
            P(),
            P("fsdp", "tp"),
            P("tp"),
            P("fsdp", "tp"),
            P(),
        ),
        check_vma=False,
    )
```

profile of v0, /device:TPU:0, one launch (start us, length us, event | category | flops | bytes accessed | tf_op | source)
XLA Modules:
  0.0 1341.5 jit_solution(14886706895732890239)
XLA Ops:
  18.1 22.4 %all-gather.15.cloned.1.call-done = bf16[2048,512]{1,0:T(8,128)(2,1)} async-done(((bf16[256,512]{1,0:T(8,128)(2,1)}), bf16[2048,512]{1,0:T(8,128)(2,1)}) %all-gather.15.cloned.1.call-update) | async-done | bytes 2097168 | tf_op jit(solution)/shard_map/all_gather | solution.py:187
  40.6 82.9 %all-gather.11.cloned.1.call-done = bf16[1024,2048]{1,0:T(8,128)(2,1)} async-done(((bf16[256,2048]{1,0:T(8,128)(2,1)}), bf16[1024,2048]{1,0:T(8,128)(2,1)}) %all-gather.11.cloned.1.call-update) | async-done | bytes 4194320 | tf_op jit(solution)/shard_map/all_gather | solution.py:200
  128.7 22.9 %all-gather.17.cloned.1.call-done = bf16[2048,512]{1,0:T(8,128)(2,1)} async-done(((bf16[256,512]{1,0:T(8,128)(2,1)}), bf16[2048,512]{1,0:T(8,128)(2,1)}) %all-gather.17.cloned.1.call-update) | async-done | bytes 2097168 | tf_op jit(solution)/shard_map/all_gather | solution.py:188
  157.9 23.3 %all-gather.13.cloned.1.call-done = bf16[2048,512]{1,0:T(8,128)(2,1)} async-done(((bf16[256,512]{1,0:T(8,128)(2,1)}), bf16[2048,512]{1,0:T(8,128)(2,1)}) %all-gather.13.cloned.1.call-update) | async-done | bytes 2097168 | tf_op jit(solution)/shard_map/all_gather | solution.py:186
  187.5 34.3 %while.45 = (s32[]{:T(128)}, bf16[2,512,8,64]{1,3,2,0:T(8,128)(2,1)}, f32[2,8,512]{2,1,0:T(8,128)S(1)}, s32[2]{0:T(128)S(1)}, bf16[8,8]{1,0:T(8,128)(2,1)S(1)}, ...) while((s32[]{:T(128)}, ...), condition=%wide.region_9.10_spmd.clone, body=%wide.region_6.9_spmd.clone.sunk | while | flops 1123386368 | bytes 68315536 | solution.py:99
  232.1 76.1 %reduce-scatter.11.cloned.1.call-done = bf16[256,2048]{1,0:T(8,128)(2,1)} async-done(((bf16[1024,2048]{1,0:T(8,128)(2,1)}), bf16[256,2048]{1,0:T(8,128)(2,1)}) %reduce-scatter.11.cloned.1.call-update) | async-done | bytes 1048592 | tf_op jit(solution)/shard_map/reduce_scatter | solution.py:155
  313.0 51.9 %all-gather.23.cloned.1.call-done = bf16[2048,2048]{1,0:T(8,128)(2,1)} async-done(((bf16[256,2048]{1,0:T(8,128)(2,1)}), bf16[2048,2048]{1,0:T(8,128)(2,1)}) %all-gather.23.cloned.1.call-update) | async-done | bytes 8388624 | tf_op jit(solution)/shard_map/all_gather | solution.py:194
  364.9 82.9 %all-gather.21.cloned.1.call-done = bf16[1024,2048]{1,0:T(8,128)(2,1)} async-done(((bf16[256,2048]{1,0:T(8,128)(2,1)}), bf16[1024,2048]{1,0:T(8,128)(2,1)}) %all-gather.21.cloned.1.call-update) | async-done | bytes 4194320 | tf_op jit(solution)/shard_map/all_gather | solution.py:216
  447.8 14.0 %maximum_convert_fusion = bf16[1024,2048]{1,0:T(8,128)(2,1)} fusion(f32[2048]{0:T(1024)S(1)} %copy-done.46, bf16[1024,2048]{1,0:T(8,128)(2,1)} %all-gather.21.cloned.1.call-done, bf16[2048,2048]{1,0:T(8,128)(2,1)} %all-gather.23.cloned.1.call-done), kind=kOutput, calls=%fused_computation.104 | convolution fusion | flops 8596226048 | bytes 16785408 | tf_op jit(solution)/shard_map/dot_general | solution.py:219
  461.8 40.7 %all-gather.25.cloned.1.call-done = bf16[2048,2048]{1,0:T(8,128)(2,1)} async-done(((bf16[256,2048]{1,0:T(8,128)(2,1)}), bf16[2048,2048]{1,0:T(8,128)(2,1)}) %all-gather.25.cloned.1.call-update) | async-done | bytes 8388624 | tf_op jit(solution)/shard_map/all_gather | solution.py:195
  502.4 13.9 %convolution_convert_fusion.4 = bf16[1024,2048]{1,0:T(8,128)(2,1)} fusion(bf16[1024,2048]{1,0:T(8,128)(2,1)} %maximum_convert_fusion, bf16[2048,2048]{1,0:T(8,128)(2,1)} %all-gather.25.cloned.1.call-done), kind=kOutput, calls=%fused_computation.108 | convolution fusion | flops 8592031744 | bytes 16777216 | tf_op jit(solution)/shard_map/dot_general | solution.py:66
  517.6 44.5 %psum.78 = f32[]{:T(128)} all-reduce(f32[]{:T(128)} %convert_reduce_fusion.7), channel_id=1, replica_groups=mesh['fsdp'=8,'tp'=4] {'fsdp','tp'}, use_global_device_ids=true, to_apply=%region_17.18 | all-reduce | flops 1 | bytes 8 | tf_op jit(solution)/shard_map/psum | solution.py:225
  562.8 31.5 %reduce-scatter.13.cloned.1.call-done = bf16[256,2048]{1,0:T(8,128)(2,1)} async-done(((bf16[1024,2048]{1,0:T(8,128)(2,1)}), bf16[256,2048]{1,0:T(8,128)(2,1)}) %reduce-scatter.13.cloned.1.call-update) | async-done | bytes 1048592 | tf_op jit(solution)/shard_map/reduce_scatter | solution.py:155
  598.9 81.3 %all-gather.27.cloned.1.call-done = bf16[1024,2048]{1,0:T(8,128)(2,1)} async-done(((bf16[256,2048]{1,0:T(8,128)(2,1)}), bf16[1024,2048]{1,0:T(8,128)(2,1)}) %all-gather.27.cloned.1.call-update) | async-done | bytes 4194320 | tf_op jit(solution)/shard_map/all_gather | solution.py:232
  680.1 14.2 %convert_reduce_fusion = (f32[2048]{0:T(1024)}, bf16[1024,2048]{1,0:T(8,128)(2,1)S(1)}) fusion(bf16[1024,2048]{1,0:T(8,128)(2,1)} %all-gather.27.cloned.1.call-done, bf16[2048,2048]{1,0:T(8,128)(2,1)} %all-gather.25.cloned.1.call-done, bf16[1024,2048]{1,0:T(8,128)(2,1)} %maximum_convert_fusion), kind=kOutput, calls=%fused_computation.101 | convolution fusion | flops 8600418304 | bytes 20979712 | tf_op jit(solution)/shard_map/dot_general | solution.py:236
  696.4 12.6 convolution_convert_fusion.3
  709.0 75.4 %reduce-scatter.15.cloned.1.call-done = bf16[256,2048]{1,0:T(8,128)(2,1)} async-done(((bf16[1024,2048]{1,0:T(8,128)(2,1)}), bf16[256,2048]{1,0:T(8,128)(2,1)}) %reduce-scatter.15.cloned.1.call-update) | async-done | bytes 1048592 | tf_op jit(solution)/shard_map/reduce_scatter | solution.py:155
  794.2 14.2 %convolution_convert_fusion.1 = bf16[2048,2048]{1,0:T(8,128)(2,1)} fusion(bf16[1024,2048]{1,0:T(8,128)(2,1)} %all-gather.27.cloned.1.call-done, bf16[1024,2048]{1,0:T(8,128)(2,1)} %maximum_convert_fusion), kind=kOutput, calls=%fused_computation.105 | convolution fusion | flops 8594128896 | bytes 16777216 | tf_op jit(solution)/shard_map/dot_general | solution.py:66
  808.5 14.1 %convolution_convert_fusion.2 = bf16[2048,2048]{1,0:T(8,128)(2,1)} fusion(bf16[1024,2048]{1,0:T(8,128)(2,1)} %all-gather.21.cloned.1.call-done, bf16[1024,2048]{1,0:T(8,128)(2,1)} %copy-done.50), kind=kOutput, calls=%fused_computation.106 | convolution fusion | flops 8594128896 | bytes 16777216 | tf_op jit(solution)/shard_map/dot_general | solution.py:66
  822.7 52.9 %all-gather.29.cloned.1.call-done = bf16[1024,2048]{1,0:T(8,128)(2,1)} async-done(((bf16[256,2048]{1,0:T(8,128)(2,1)}), bf16[1024,2048]{1,0:T(8,128)(2,1)}) %all-gather.29.cloned.1.call-update) | async-done | bytes 4194320 | tf_op jit(solution)/shard_map/all_gather | solution.py:251
  881.9 6.9 convolution_convert_fusion.10
  889.8 105.0 %while.47 = (s32[]{:T(128)}, f32[1024,8,64]{0,2,1:T(8,128)S(1)}, f32[1024,8,64]{0,2,1:T(8,128)}, bf16[2,512,8,64]{1,3,2,0:T(8,128)(2,1)}, s32[2]{0:T(128)S(1)}, ...) while((s32[]{:T(128)}, f32[1024,8,64]{0,2,1:T(8,128)S(1)}, ...), condition=%wide.region_23.24_spmd.clone, body=%wide.region_21.23_spmd.clone.sunk | while | flops 2748679168 | bytes 224012784 | solution.py:143
  910.9 12.9 multiply_reduce_fusion.4
  923.8 12.7 multiply_convert_fusion.4
  961.8 14.7 %multiply_reduce_fusion.4 = (f32[8,512]{1,0:T(8,128)S(1)}, f32[8,512,1024]{2,1,0:T(8,128)}) fusion(f32[8,512,1024]{2,1,0:T(8,128)} %copy-done, f32[8,512]{1,0:T(8,128)S(1)} %dynamic-slice_bitcast_fusion.2, pred[512,1024]{1,0:T(8,128)(4,1)S(1)} %copy-done.4, bf16[1024,8,64]{0,2,1:T(8,128)(2,1)} %get-tuple-element.828, ...), kind=kOutput, calls=%fused_computation.51.clone.1 | convolution fusion | flops 553644032 | bytes 35684356 | tf_op jit(solution)/shard_map/while/body/eval_jaxpr/qhd,khd->hqk/dot_general | solution.py:122
  976.5 13.2 multiply_convert_fusion.4
  1038.1 30.0 %reduce-scatter.25.cloned.1.call-done = bf16[256,512]{1,0:T(8,128)(2,1)} async-done(((bf16[2048,512]{1,0:T(8,128)(2,1)}), bf16[256,512]{1,0:T(8,128)(2,1)}) %reduce-scatter.25.cloned.1.call-update) | async-done | bytes 262160 | tf_op jit(solution)/shard_map/reduce_scatter | solution.py:155
  1069.9 42.5 %reduce-scatter.23.cloned.1.call-done = bf16[256,512]{1,0:T(8,128)(2,1)} async-done(((bf16[2048,512]{1,0:T(8,128)(2,1)}), bf16[256,512]{1,0:T(8,128)(2,1)}) %reduce-scatter.23.cloned.1.call-update) | async-done | bytes 262160 | tf_op jit(solution)/shard_map/reduce_scatter | solution.py:155
  1114.2 42.5 %reduce-scatter.19.cloned.1.call-done = bf16[256,512]{1,0:T(8,128)(2,1)} async-done(((bf16[2048,512]{1,0:T(8,128)(2,1)}), bf16[256,512]{1,0:T(8,128)(2,1)}) %reduce-scatter.19.cloned.1.call-update) | async-done | bytes 262160 | tf_op jit(solution)/shard_map/reduce_scatter | solution.py:155
  1158.4 42.6 %reduce-scatter.21.cloned.1.call-done = bf16[256,512]{1,0:T(8,128)(2,1)} async-done(((bf16[2048,512]{1,0:T(8,128)(2,1)}), bf16[256,512]{1,0:T(8,128)(2,1)}) %reduce-scatter.21.cloned.1.call-update) | async-done | bytes 262160 | tf_op jit(solution)/shard_map/reduce_scatter | solution.py:155
  1202.9 77.1 %reduce-scatter.17.cloned.1.call-done = bf16[256,2048]{1,0:T(8,128)(2,1)} async-done(((bf16[1024,2048]{1,0:T(8,128)(2,1)}), bf16[256,2048]{1,0:T(8,128)(2,1)}) %reduce-scatter.17.cloned.1.call-update) | async-done | bytes 1048592 | tf_op jit(solution)/shard_map/reduce_scatter | solution.py:155
  1284.3 43.1 %all-reduce.2 = (f32[]{:T(128)}, f32[2048]{0:T(1024)}, f32[2048]{0:T(1024)}, f32[2048]{0:T(1024)S(1)}, f32[2048]{0:T(1024)S(1)}, /*index=5*/f32[2048]{0:T(1024)}...) all-reduce(f32[]{:T(128)} %get-tuple-element.543, ...), channel_id=1, replica_groups=mesh['fsdp'=8,'tp'=4] {'fsdp','tp'}, use_global_device_ids=true, to_apply=%region_15.16 | all-reduce | flops 24577 | bytes 196616 | tf_op jit(solution)/shard_map/psum | solution.py:225
  (296 shorter events, 206.4 us)
Async XLA Ops:
  7.2 33.3 %all-gather.15.cloned.1.call-start = ((), (), s32[]{:S(2)}) async-start(), calls=%async_computation.12 | async-start | bytes 2359296 | tf_op jit(solution)/shard_map/all_gather | solution.py:187
  8.0 115.5 %all-gather.11.cloned.1.call-start = ((), (), s32[]{:S(2)}) async-start(), calls=%async_computation.10 | async-start | bytes 5242880 | tf_op jit(solution)/shard_map/all_gather | solution.py:200
  13.7 137.9 %all-gather.17.cloned.1.call-start = ((), (), s32[]{:S(2)}) async-start(), calls=%async_computation.13 | async-start | bytes 2359296 | tf_op jit(solution)/shard_map/all_gather | solution.py:188
  14.5 166.8 %all-gather.13.cloned.1.call-start = ((), (), s32[]{:S(2)}) async-start(), calls=%async_computation.11 | async-start | bytes 2359296 | tf_op jit(solution)/shard_map/all_gather | solution.py:186
  15.0 209.8 %all-gather.19.cloned.1.call-start = ((), (), s32[]{:S(2)}) async-start(), calls=%async_computation.14 | async-start | bytes 2359296 | tf_op jit(solution)/shard_map/all_gather | solution.py:189
  15.6 292.6 %reduce-scatter.11.cloned.1.call-start = ((), (), s32[]{:S(2)}) async-start(), calls=%async_computation.15 | async-start | bytes 5242880 | tf_op jit(solution)/shard_map/reduce_scatter | solution.py:155
  18.1 133.5 %copy-start.47 = (f32[512]{0:T(512)S(1)}, f32[512]{0:T(512)}, u32[]{:S(2)}) copy-start(f32[512]{0:T(512)} %param.33) | copy-start | bytes 6148
  231.2 133.6 %all-gather.23.cloned.1.call-start = ((), (), s32[]{:S(2)}) async-start(), calls=%async_computation.17 | async-start | bytes 9437184 | tf_op jit(solution)/shard_map/all_gather | solution.py:194
  232.0 215.8 %all-gather.21.cloned.1.call-start = ((), (), s32[]{:S(2)}) async-start(), calls=%async_computation.16 | async-start | bytes 5242880 | tf_op jit(solution)/shard_map/all_gather | solution.py:216
  310.5 137.2 %copy-start.46 = (f32[2048]{0:T(1024)S(1)}, f32[2048]{0:T(1024)}, u32[]{:S(2)}) copy-start(f32[2048]{0:T(1024)} %param.39) | copy-start | bytes 24580
  312.2 190.2 %all-gather.25.cloned.1.call-start = ((), (), s32[]{:S(2)}) async-start(), calls=%async_computation.18 | async-start | bytes 9437184 | tf_op jit(solution)/shard_map/all_gather | solution.py:195
  313.0 281.4 %reduce-scatter.13.cloned.1.call-start = ((), (), s32[]{:S(2)}) async-start(), calls=%async_computation.19 | async-start | bytes 5242880 | tf_op jit(solution)/shard_map/reduce_scatter | solution.py:155
  516.4 163.8 %all-gather.27.cloned.1.call-start = ((), (), s32[]{:S(2)}) async-start(), calls=%async_computation.20 | async-start | bytes 5242880 | tf_op jit(solution)/shard_map/all_gather | solution.py:232
  598.8 185.6 %reduce-scatter.15.cloned.1.call-start = ((), (), s32[]{:S(2)}) async-start(), calls=%async_computation.21 | async-start | bytes 5242880 | tf_op jit(solution)/shard_map/reduce_scatter | solution.py:155
  709.0 166.6 %all-gather.29.cloned.1.call-start = ((), (), s32[]{:S(2)}) async-start(), calls=%async_computation.22 | async-start | bytes 5242880 | tf_op jit(solution)/shard_map/all_gather | solution.py:251
  794.2 237.2 %reduce-scatter.29.cloned.1.call-start = ((), (), s32[]{:S(2)}) async-start(), calls=%async_computation.29 | async-start | bytes 9437184 | tf_op jit(solution)/shard_map/reduce_scatter | solution.py:243
  808.5 225.8 %reduce-scatter.27.cloned.1.call-start = ((), (), s32[]{:S(2)}) async-start(), calls=%async_computation.28 | async-start | bytes 9437184 | tf_op jit(solution)/shard_map/reduce_scatter | solution.py:240
  822.6 245.5 %reduce-scatter.25.cloned.1.call-start = ((), (), s32[]{:S(2)}) async-start(), calls=%async_computation.27 | async-start | bytes 2359296 | tf_op jit(solution)/shard_map/reduce_scatter | solution.py:155
  881.8 230.5 %reduce-scatter.23.cloned.1.call-start = ((), (), s32[]{:S(2)}) async-start(), calls=%async_computation.26 | async-start | bytes 2359296 | tf_op jit(solution)/shard_map/reduce_scatter | solution.py:155
  1003.7 152.9 %reduce-scatter.19.cloned.1.call-start = ((), (), s32[]{:S(2)}) async-start(), calls=%async_computation.24 | async-start | bytes 2359296 | tf_op jit(solution)/shard_map/reduce_scatter | solution.py:155
  1011.2 189.9 %reduce-scatter.21.cloned.1.call-start = ((), (), s32[]{:S(2)}) async-start(), calls=%async_computation.25 | async-start | bytes 2359296 | tf_op jit(solution)/shard_map/reduce_scatter | solution.py:155
  1017.4 262.6 %reduce-scatter.17.cloned.1.call-start = ((), (), s32[]{:S(2)}) async-start(), calls=%async_computation.23 | async-start | bytes 5242880 | tf_op jit(solution)/shard_map/reduce_scatter | solution.py:155
  1037.2 242.9 %copy-start.3 = (bf16[256,2048]{1,0:T(8,128)(2,1)S(1)}, bf16[256,2048]{1,0:T(8,128)(2,1)}, u32[]{:S(2)}) copy-start(bf16[256,2048]{1,0:T(8,128)(2,1)} %param.26) | copy-start | bytes 3145732
  1037.2 242.9 %copy-start.26 = (f32[2048]{0:T(1024)S(1)}, f32[2048]{0:T(1024)}, u32[]{:S(2)}) copy-start(f32[2048]{0:T(1024)} %param.27) | copy-start | bytes 24580
  1037.2 242.9 %copy-start.29 = (f32[256]{0:T(256)S(1)}, f32[256]{0:T(256)}, u32[]{:S(2)}) copy-start(f32[256]{0:T(256)} %copy-done.28) | copy-start | bytes 3076
  1069.9 212.1 %copy-start.37 = (f32[256]{0:T(256)S(1)}, f32[256]{0:T(256)}, u32[]{:S(2)}) copy-start(f32[256]{0:T(256)} %copy-done.36) | copy-start | bytes 3076
  1069.9 212.1 %copy-start.35 = (f32[256]{0:T(256)S(1)}, f32[256]{0:T(256)}, u32[]{:S(2)}) copy-start(f32[256]{0:T(256)} %copy-done.34) | copy-start | bytes 3076
  1202.9 81.4 %copy-start.30 = (f32[2048]{0:T(1024)S(1)}, f32[2048]{0:T(1024)}, u32[]{:S(2)}) copy-start(f32[2048]{0:T(1024)} %get-tuple-element.460) | copy-start | bytes 24580
  1202.9 81.4 %copy-start.31 = (f32[2048]{0:T(1024)S(1)}, f32[2048]{0:T(1024)}, u32[]{:S(2)}) copy-start(f32[2048]{0:T(1024)} %get-tuple-element.454) | copy-start | bytes 24580
  1202.9 81.4 %copy-start.32 = (f32[2048]{0:T(1024)S(1)}, f32[2048]{0:T(1024)}, u32[]{:S(2)}) copy-start(f32[2048]{0:T(1024)} %get-tuple-element.528) | copy-start | bytes 24580
  1202.9 81.4 %copy-start.33 = (f32[2048]{0:T(1024)S(1)}, f32[2048]{0:T(1024)}, u32[]{:S(2)}) copy-start(f32[2048]{0:T(1024)} %get-tuple-element.544) | copy-start | bytes 24580
  1202.9 127.1 %copy-start.10 = (f32[256,2048]{1,0:T(8,128)S(1)}, f32[256,2048]{1,0:T(8,128)}, u32[]{:S(2)}) copy-start(f32[256,2048]{1,0:T(8,128)} %copy-done.9) | copy-start | bytes 6291460
  (47 other events, 600.2 us)
Sparse Core Ops, SparseCore 0:
  9.9 30.5 all-gather.14
  42.7 80.7 all-gather.10
  125.4 26.2 all-gather.16
  153.4 27.7 all-gather.12
  183.0 27.7 all-gather.18
  231.4 76.7 reduce-scatter.10
  310.1 54.7 all-gather.22
  367.0 80.7 all-gather.20
  449.7 52.7 all-gather.24
  516.5 77.8 reduce-scatter.12
  598.9 81.1 all-gather.26
  709.1 75.2 reduce-scatter.14
  794.3 81.2 all-gather.28
  878.9 69.9 reduce-scatter.28
  952.2 71.5 reduce-scatter.26
  1026.9 41.1 reduce-scatter.24
  1071.2 41.1 reduce-scatter.22
  1115.5 41.1 reduce-scatter.18
  1159.9 41.1 reduce-scatter.20
  1203.2 76.7 reduce-scatter.16
where the time goes:
time: 1350 us; the launch traced here: 1340 us
  waiting for transfers between devices  883 us (65%)
  matrix products  225 us (17%)
  blocking collectives  87.6 us (6%)
  other arithmetic  83.4 us (6%)
  local copies, waits for them, and re-layouts  33.8 us (3%)
  between operations  18.2 us (1%)
    reduce_scatter x8, waiting for transfers between devices, scatter_narrow(): lax.psum_scatter(partial_sums.astype(jnp.bfloat16), axis, scatter_dimensi...  418 us
    dot_general x12, matrix products, contract(): lax.dot_general(left_side, right_side, (((left_dim,), (right_dim,)), ((),...  95.7 us
    psum x2, blocking collectives, body(): lax.psum((jnp.sum(weight_mask), jnp.sum(weight_mask[:, None] * deviation...  87.6 us
    all_gather x1, waiting for transfers between devices, body(): normed_all = lax.all_gather(normed, 'tp', axis=0, tiled=True)  82.9 us
    all_gather x1, waiting for transfers between devices, body(): normed_mid_all = lax.all_gather(normed_mid, 'tp', axis=0, tiled=True)  82.9 us
    all_gather x1, waiting for transfers between devices, body(): lax.all_gather(grad_output.astype(jnp.bfloat16), 'tp', axis=0, tiled=True)  81.3 us
    all_gather x1, waiting for transfers between devices, body(): lax.all_gather(grad_hidden.astype(jnp.bfloat16), 'tp', axis=0, tiled=True)  52.9 us
    all_gather x1, waiting for transfers between devices, feed_weights(): lax.all_gather(w_up, 'fsdp', axis=0, tiled=True)  51.9 us
  transfers between devices with their start and end apart: 20, of which 17 were waited for; matrix products, arithmetic and copies ran while one was open for 19% of the time, Pallas kernels for 0%

commit v1 on v0

--- a/solution.py
+++ b/solution.py
@@ -6,6 +6,33 @@
 HD = 64
 EPSILON = 1e-05
 MASKED_SCORE = -1e30
+
+
+def pages_handle(t0, array_dim):
+    everything, y2, step_out = (
+        jax.lax.axis_size("fsdp"),
+        jax.lax.axis_index("fsdp"),
+        t0.shape[array_dim],
+    )
+    no = 1
+    moved = lax.dynamic_update_slice_in_dim(
+        jnp.zeros(
+            [it * everything if to_i == array_dim else it for to_i, it in enumerate(t0.shape)],
+            t0.dtype,
+        ),
+        t0,
+        y2 * step_out,
+        axis=array_dim,
+    )
+    while no < everything:
+        t0 = jax.lax.ppermute(
+            t0, "fsdp", [(to_i, (to_i + 1) % everything) for to_i in range(everything)]
+        )
+        moved = lax.dynamic_update_slice_in_dim(
+            moved, t0, (y2 - no) % everything * step_out, axis=array_dim
+        )
+        no += 1
+    return moved
 
 
 def layer_norm(vectors, norm_gain, norm_shift):
@@ -190,10 +217,7 @@
         )
 
     def feed_weights():
-        return (
-            lax.all_gather(w_up, "fsdp", axis=0, tiled=True),
-            lax.all_gather(w_down, "fsdp", axis=0, tiled=True),
-        )
+        return (lax.all_gather(w_up, "fsdp", axis=0, tiled=True), pages_handle(w_down, array_dim=0))
 
     inputs = tokens.astype(jnp.float32)
     normed = layer_norm(inputs, norm1_gain, norm1_shift).astype(jnp.bfloat16)

time: 1350 us -> 1320 us (0.978)
  waiting for transfers between devices: 883 us -> 835 us
  local copies, waits for them, and re-layouts: 33.8 us -> 56.5 us
    ppermute x0 -> x7, waiting for transfers between devices: none -> 103 us  [pages_handle(): jax.lax.ppermute(t0, 'fsdp', [(to_i, (to_i + 1) % everything) for to_i in...]
    all_gather x1, waiting for transfers between devices: 51.9 us -> 0.01 us  [feed_weights(): lax.all_gather(w_up, 'fsdp', axis=0, tiled=True)]
    all_gather x1, waiting for transfers between devices: 82.9 us -> 41.4 us  [body(): normed_mid_all = lax.all_gather(normed_mid, 'tp', axis=0, tiled=True)]
    all_gather x1 -> x0, waiting for transfers between devices: 40.7 us -> none  [feed_weights(): lax.all_gather(w_down, 'fsdp', axis=0, tiled=True)]
    reduce_scatter x8, waiting for transfers between devices: 418 us -> 402 us  [scatter_narrow(): lax.psum_scatter(partial_sums.astype(jnp.bfloat16), axis, scatter_dimensi...]
    dynamic_update_slice x0 -> x8, local copies, waits for them, and re-layouts: none -> 13.6 us  [the longest x7 12.5 us: pages_handle(): lax.dynamic_update_slice_in_dim(moved, t0, (y2 - no) % everything * step_...]
  transfers between devices with their start and end apart: 20 -> 26, of which waited for: 17 -> 21; matrix products, arithmetic and copies ran while one was open for 19% -> 19% of each run, Pallas kernels for 0% -> 0%
where the time goes in v1:
time: 1320 us; the launch traced here: 1310 us
  waiting for transfers between devices  835 us (63%)
  matrix products  222 us (17%)
  blocking collectives  86.9 us (7%)
  other arithmetic  82.9 us (6%)
  local copies, waits for them, and re-layouts  56.5 us (4%)
  between operations  18.3 us (1%)
    reduce_scatter x8, waiting for transfers between devices, scatter_narrow(): lax.psum_scatter(partial_sums.astype(jnp.bfloat16), axis, scatter_dimensi...  402 us
    ppermute x7, waiting for transfers between devices, pages_handle(): jax.lax.ppermute(t0, 'fsdp', [(to_i, (to_i + 1) % everything) for to_i in...  103 us
    dot_general x12, matrix products, contract(): lax.dot_general(left_side, right_side, (((left_dim,), (right_dim,)), ((),...  94.3 us
    psum x2, blocking collectives, body(): lax.psum((jnp.sum(weight_mask), jnp.sum(weight_mask[:, None] * deviation...  86.9 us
    all_gather x1, waiting for transfers between devices, body(): normed_all = lax.all_gather(normed, 'tp', axis=0, tiled=True)  82.9 us
    all_gather x1, waiting for transfers between devices, body(): lax.all_gather(grad_output.astype(jnp.bfloat16), 'tp', axis=0, tiled=True)  81.1 us
    all_gather x1, waiting for transfers between devices, body(): lax.all_gather(grad_hidden.astype(jnp.bfloat16), 'tp', axis=0, tiled=True)  52.6 us
    all_gather x1, waiting for transfers between devices, body(): normed_mid_all = lax.all_gather(normed_mid, 'tp', axis=0, tiled=True)  41.4 us
  transfers between devices with their start and end apart: 26, of which 21 were waited for; matrix products, arithmetic and copies ran while one was open for 19% of the time, Pallas kernels for 0%

profile of v1, /device:TPU:0, one launch (start us, length us, event | category | flops | bytes accessed | tf_op | source)
XLA Modules:
  0.0 1313.1 jit_solution(14491920027160919450)
XLA Ops:
  18.1 22.4 %all-gather.14.cloned.1.call-done = bf16[2048,512]{1,0:T(8,128)(2,1)} async-done(((bf16[256,512]{1,0:T(8,128)(2,1)}), bf16[2048,512]{1,0:T(8,128)(2,1)}) %all-gather.14.cloned.1.call-update) | async-done | bytes 2097168 | tf_op jit(solution)/shard_map/all_gather | solution.py:214
  40.6 82.9 %all-gather.10.cloned.1.call-done = bf16[1024,2048]{1,0:T(8,128)(2,1)} async-done(((bf16[256,2048]{1,0:T(8,128)(2,1)}), bf16[1024,2048]{1,0:T(8,128)(2,1)}) %all-gather.10.cloned.1.call-update) | async-done | bytes 4194320 | tf_op jit(solution)/shard_map/all_gather | solution.py:224
  128.7 22.9 %all-gather.16.cloned.1.call-done = bf16[2048,512]{1,0:T(8,128)(2,1)} async-done(((bf16[256,512]{1,0:T(8,128)(2,1)}), bf16[2048,512]{1,0:T(8,128)(2,1)}) %all-gather.16.cloned.1.call-update) | async-done | bytes 2097168 | tf_op jit(solution)/shard_map/all_gather | solution.py:215
  157.9 23.3 %all-gather.12.cloned.1.call-done = bf16[2048,512]{1,0:T(8,128)(2,1)} async-done(((bf16[256,512]{1,0:T(8,128)(2,1)}), bf16[2048,512]{1,0:T(8,128)(2,1)}) %all-gather.12.cloned.1.call-update) | async-done | bytes 2097168 | tf_op jit(solution)/shard_map/all_gather | solution.py:213
  187.5 34.4 %while.45 = (s32[]{:T(128)}, bf16[2,512,8,64]{1,3,2,0:T(8,128)(2,1)}, f32[2,8,512]{2,1,0:T(8,128)S(1)}, s32[2]{0:T(128)S(1)}, bf16[8,8]{1,0:T(8,128)(2,1)S(1)}, ...) while((s32[]{:T(128)}, ...), condition=%wide.region_9.10_spmd.clone, body=%wide.region_6.9_spmd.clone.sunk | while | flops 1123386368 | bytes 68315536 | solution.py:126
  233.2 15.0 %collective-permute-done = bf16[256,2048]{1,0:T(8,128)(2,1)} collective-permute-done((bf16[256,2048]{1,0:T(8,128)(2,1)S(1)}, bf16[256,2048]{1,0:T(8,128)(2,1)}, u32[]{:S(2)}, u32[]{:S(2)}) %collective-permute-start) | collective-permute-done | bytes 1048608 | tf_op jit(solution)/shard_map/ppermute | solution.py:28
  248.2 60.5 %reduce-scatter.11.cloned.1.call-done = bf16[256,2048]{1,0:T(8,128)(2,1)} async-done(((bf16[1024,2048]{1,0:T(8,128)(2,1)}), bf16[256,2048]{1,0:T(8,128)(2,1)}) %reduce-scatter.11.cloned.1.call-update) | async-done | bytes 1048592 | tf_op jit(solution)/shard_map/reduce_scatter | solution.py:182
  313.3 26.6 %collective-permute-done.2 = bf16[256,2048]{1,0:T(8,128)(2,1)S(1)} collective-permute-done((bf16[256,2048]{1,0:T(8,128)(2,1)}, bf16[256,2048]{1,0:T(8,128)(2,1)S(1)}, u32[]{:S(2)}, u32[]{:S(2)}) %collective-permute-start.2) | collective-permute-done | bytes 1048608 | tf_op jit(solution)/shard_map/ppermute | solution.py:28
  340.8 32.6 %collective-permute-done.3 = bf16[256,2048]{1,0:T(8,128)(2,1)S(1)} collective-permute-done((bf16[256,2048]{1,0:T(8,128)(2,1)S(1)}, bf16[256,2048]{1,0:T(8,128)(2,1)S(1)}, u32[]{:S(2)}, u32[]{:S(2)}) %collective-permute-start.3) | collective-permute-done | bytes 1048608 | tf_op jit(solution)/shard_map/ppermute | solution.py:28
  374.4 15.4 %collective-permute-done.4 = bf16[256,2048]{1,0:T(8,128)(2,1)} collective-permute-done((bf16[256,2048]{1,0:T(8,128)(2,1)S(1)}, bf16[256,2048]{1,0:T(8,128)(2,1)}, u32[]{:S(2)}, u32[]{:S(2)}) %collective-permute-start.4) | collective-permute-done | bytes 1048608 | tf_op jit(solution)/shard_map/ppermute | solution.py:28
  421.6 41.4 %all-gather.20.cloned.1.call-done = bf16[1024,2048]{1,0:T(8,128)(2,1)} async-done(((bf16[256,2048]{1,0:T(8,128)(2,1)}), bf16[1024,2048]{1,0:T(8,128)(2,1)}) %all-gather.20.cloned.1.call-update) | async-done | bytes 4194320 | tf_op jit(solution)/shard_map/all_gather | solution.py:240
  477.4 12.6 convolution_convert_fusion.4
  491.3 43.7 %psum.78 = f32[]{:T(128)} all-reduce(f32[]{:T(128)} %convert_reduce_fusion.7), channel_id=1, replica_groups=mesh['fsdp'=8,'tp'=4] {'fsdp','tp'}, use_global_device_ids=true, to_apply=%region_17.18 | all-reduce | flops 1 | bytes 8 | tf_op jit(solution)/shard_map/psum | solution.py:249
  535.8 30.8 %reduce-scatter.13.cloned.1.call-done = bf16[256,2048]{1,0:T(8,128)(2,1)} async-done(((bf16[1024,2048]{1,0:T(8,128)(2,1)}), bf16[256,2048]{1,0:T(8,128)(2,1)}) %reduce-scatter.13.cloned.1.call-update) | async-done | bytes 1048592 | tf_op jit(solution)/shard_map/reduce_scatter | solution.py:182
  570.9 81.1 %all-gather.24.cloned.1.call-done = bf16[1024,2048]{1,0:T(8,128)(2,1)} async-done(((bf16[256,2048]{1,0:T(8,128)(2,1)}), bf16[1024,2048]{1,0:T(8,128)(2,1)}) %all-gather.24.cloned.1.call-update) | async-done | bytes 4194320 | tf_op jit(solution)/shard_map/all_gather | solution.py:256
  652.0 13.8 %convert_reduce_fusion = (f32[2048]{0:T(1024)}, bf16[1024,2048]{1,0:T(8,128)(2,1)S(1)}) fusion(bf16[1024,2048]{1,0:T(8,128)(2,1)} %all-gather.24.cloned.1.call-done, bf16[2048,2048]{1,0:T(8,128)(2,1)} %constant_dynamic-update-slice_fusion, bf16[1024,2048]{1,0:T(8,128)(2,1)} %copy-done.69), kind=kOutput, calls=%fused_computation.101 | convolution fusion | flops 8600418304 | bytes 20979712 | tf_op jit(solution)/shard_map/dot_general | solution.py:260
  667.8 12.6 convolution_convert_fusion.3
  680.5 75.4 %reduce-scatter.15.cloned.1.call-done = bf16[256,2048]{1,0:T(8,128)(2,1)} async-done(((bf16[1024,2048]{1,0:T(8,128)(2,1)}), bf16[256,2048]{1,0:T(8,128)(2,1)}) %reduce-scatter.15.cloned.1.call-update) | async-done | bytes 1048592 | tf_op jit(solution)/shard_map/reduce_scatter | solution.py:182
  766.2 14.1 %convolution_convert_fusion.1 = bf16[2048,2048]{1,0:T(8,128)(2,1)} fusion(bf16[1024,2048]{1,0:T(8,128)(2,1)} %all-gather.24.cloned.1.call-done, bf16[1024,2048]{1,0:T(8,128)(2,1)} %copy-done.69), kind=kOutput, calls=%fused_computation.105 | convolution fusion | flops 8594128896 | bytes 16777216 | tf_op jit(solution)/shard_map/dot_general | solution.py:93
  780.3 14.1 %convolution_convert_fusion.2 = bf16[2048,2048]{1,0:T(8,128)(2,1)} fusion(bf16[1024,2048]{1,0:T(8,128)(2,1)} %all-gather.20.cloned.1.call-done, bf16[1024,2048]{1,0:T(8,128)(2,1)} %copy-done.70), kind=kOutput, calls=%fused_computation.106 | convolution fusion | flops 8594128896 | bytes 16777216 | tf_op jit(solution)/shard_map/dot_general | solution.py:93
  794.5 52.6 %all-gather.26.cloned.1.call-done = bf16[1024,2048]{1,0:T(8,128)(2,1)} async-done(((bf16[256,2048]{1,0:T(8,128)(2,1)}), bf16[1024,2048]{1,0:T(8,128)(2,1)}) %all-gather.26.cloned.1.call-update) | async-done | bytes 4194320 | tf_op jit(solution)/shard_map/all_gather | solution.py:275
  861.3 104.8 %while.47 = (s32[]{:T(128)}, f32[1024,8,64]{0,2,1:T(8,128)S(1)}, f32[1024,8,64]{0,2,1:T(8,128)}, bf16[2,512,8,64]{1,3,2,0:T(8,128)(2,1)}, s32[2]{0:T(128)S(1)}, ...) while((s32[]{:T(128)}, f32[1024,8,64]{0,2,1:T(8,128)S(1)}, ...), condition=%wide.region_23.24_spmd.clone, body=%wide.region_21.23_spmd.clone.sunk | while | flops 2748679168 | bytes 224012784 | solution.py:170
  882.3 13.0 multiply_reduce_fusion.4
  895.3 12.6 multiply_convert_fusion.4
  933.2 14.9 %multiply_reduce_fusion.4 = (f32[8,512]{1,0:T(8,128)S(1)}, f32[8,512,1024]{2,1,0:T(8,128)}) fusion(f32[8,512,1024]{2,1,0:T(8,128)} %copy-done, f32[8,512]{1,0:T(8,128)S(1)} %dynamic-slice_bitcast_fusion.2, pred[512,1024]{1,0:T(8,128)(4,1)S(1)} %copy-done.6, bf16[1024,8,64]{0,2,1:T(8,128)(2,1)} %get-tuple-element.828, ...), kind=kOutput, calls=%fused_computation.51.clone.1 | convolution fusion | flops 553644032 | bytes 35684356 | tf_op jit(solution)/shard_map/while/body/eval_jaxpr/qhd,khd->hqk/dot_general | solution.py:149
  948.0 13.2 %multiply_convert_fusion.4 = bf16[8,512,1024]{2,1,0:T(8,128)(2,1)S(1)} fusion(f32[8,512,1024]{2,1,0:T(8,128)} %get-tuple-element.726, f32[8,512,1024]{2,1,0:T(8,128)} %copy-done, f32[8,512]{1,0:T(8,128)S(1)} %get-tuple-element.727, f32[8,512]{1,0:T(8,128)S(1)} %dynamic-slice_bitcast_fusion.2, pred[512,1024]{1,0:T(8,128)(4,1)S(1)} %copy-done.6), kind=kLoop, calls=%fused_computation.50.clone.1 | loop fusion | flops 20971520 | bytes 42500096 | tf_op jit(solution)/shard_map/while/body/eval_jaxpr/convert_element_type | solution.py:153
  1009.6 30.2 %reduce-scatter.25.cloned.1.call-done = bf16[256,512]{1,0:T(8,128)(2,1)} async-done(((bf16[2048,512]{1,0:T(8,128)(2,1)}), bf16[256,512]{1,0:T(8,128)(2,1)}) %reduce-scatter.25.cloned.1.call-update) | async-done | bytes 262160 | tf_op jit(solution)/shard_map/reduce_scatter | solution.py:182
  1041.6 42.5 %reduce-scatter.23.cloned.1.call-done = bf16[256,512]{1,0:T(8,128)(2,1)} async-done(((bf16[2048,512]{1,0:T(8,128)(2,1)}), bf16[256,512]{1,0:T(8,128)(2,1)}) %reduce-scatter.23.cloned.1.call-update) | async-done | bytes 262160 | tf_op jit(solution)/shard_map/reduce_scatter | solution.py:182
  1085.9 42.5 %reduce-scatter.19.cloned.1.call-done = bf16[256,512]{1,0:T(8,128)(2,1)} async-done(((bf16[2048,512]{1,0:T(8,128)(2,1)}), bf16[256,512]{1,0:T(8,128)(2,1)}) %reduce-scatter.19.cloned.1.call-update) | async-done | bytes 262160 | tf_op jit(solution)/shard_map/reduce_scatter | solution.py:182
  1130.2 42.5 %reduce-scatter.21.cloned.1.call-done = bf16[256,512]{1,0:T(8,128)(2,1)} async-done(((bf16[2048,512]{1,0:T(8,128)(2,1)}), bf16[256,512]{1,0:T(8,128)(2,1)}) %reduce-scatter.21.cloned.1.call-update) | async-done | bytes 262160 | tf_op jit(solution)/shard_map/reduce_scatter | solution.py:182
  1174.5 77.3 %reduce-scatter.17.cloned.1.call-done = bf16[256,2048]{1,0:T(8,128)(2,1)} async-done(((bf16[1024,2048]{1,0:T(8,128)(2,1)}), bf16[256,2048]{1,0:T(8,128)(2,1)}) %reduce-scatter.17.cloned.1.call-update) | async-done | bytes 1048592 | tf_op jit(solution)/shard_map/reduce_scatter | solution.py:182
  1256.0 43.1 %all-reduce.2 = (f32[]{:T(128)}, f32[2048]{0:T(1024)}, f32[2048]{0:T(1024)}, f32[2048]{0:T(1024)S(1)}, f32[2048]{0:T(1024)S(1)}, /*index=5*/f32[2048]{0:T(1024)}...) all-reduce(f32[]{:T(128)} %get-tuple-element.543, ...), channel_id=1, replica_groups=mesh['fsdp'=8,'tp'=4] {'fsdp','tp'}, use_global_device_ids=true, to_apply=%region_15.16 | all-reduce | flops 24577 | bytes 196616 | tf_op jit(solution)/shard_map/psum | solution.py:249
  (356 shorter events, 262.7 us)
Async XLA Ops:
  7.2 33.3 %all-gather.14.cloned.1.call-start = ((), (), s32[]{:S(2)}) async-start(), calls=%async_computation.12 | async-start | bytes 2359296 | tf_op jit(solution)/shard_map/all_gather | solution.py:214
  8.0 115.5 %all-gather.10.cloned.1.call-start = ((), (), s32[]{:S(2)}) async-start(), calls=%async_computation.10 | async-start | bytes 5242880 | tf_op jit(solution)/shard_map/all_gather | solution.py:224
  13.7 137.9 %all-gather.16.cloned.1.call-start = ((), (), s32[]{:S(2)}) async-start(), calls=%async_computation.13 | async-start | bytes 2359296 | tf_op jit(solution)/shard_map/all_gather | solution.py:215
  14.5 166.8 %all-gather.12.cloned.1.call-start = ((), (), s32[]{:S(2)}) async-start(), calls=%async_computation.11 | async-start | bytes 2359296 | tf_op jit(solution)/shard_map/all_gather | solution.py:213
  15.0 210.4 %all-gather.18.cloned.1.call-start = ((), (), s32[]{:S(2)}) async-start(), calls=%async_computation.14 | async-start | bytes 2359296 | tf_op jit(solution)/shard_map/all_gather | solution.py:216
  15.6 293.1 %reduce-scatter.11.cloned.1.call-start = ((), (), s32[]{:S(2)}) async-start(), calls=%async_computation.15 | async-start | bytes 5242880 | tf_op jit(solution)/shard_map/reduce_scatter | solution.py:182
  18.1 133.5 %copy-start.64 = (f32[512]{0:T(512)S(1)}, f32[512]{0:T(512)}, u32[]{:S(2)}) copy-start(f32[512]{0:T(512)} %param.33) | copy-start | bytes 6148
  231.8 189.8 %all-gather.22.cloned.1.call-start = ((), (), s32[]{:S(2)}) async-start(), calls=%async_computation.17 | async-start | bytes 9437184 | tf_op jit(solution)/shard_map/all_gather | solution.py:220
  232.6 230.3 %all-gather.20.cloned.1.call-start = ((), (), s32[]{:S(2)}) async-start(), calls=%async_computation.16 | async-start | bytes 5242880 | tf_op jit(solution)/shard_map/all_gather | solution.py:240
  233.0 15.2 %collective-permute-start = (bf16[256,2048]{1,0:T(8,128)(2,1)S(1)}, bf16[256,2048]{1,0:T(8,128)(2,1)}, u32[]{:S(2)}, u32[]{:S(2)}) collective-permute-start(bf16[256,2048]{1,0:T(8,128)(2,1)S(1)} %copy-done.24), channel_id=1, source_target_pairs={{0,4},{4,8},{8,12},{12,16},{16,20},{20,24},{24,28},{28,0},{1,5},{5... | collective-permute-start | bytes 3145736 | tf_op jit(solution)/shard_map/ppermute | solution.py:28
  248.2 64.6 %collective-permute-start.1 = (bf16[256,2048]{1,0:T(8,128)(2,1)}, bf16[256,2048]{1,0:T(8,128)(2,1)}, u32[]{:S(2)}, u32[]{:S(2)}) collective-permute-start(bf16[256,2048]{1,0:T(8,128)(2,1)} %collective-permute-done), channel_id=1, source_target_pairs={{0,4},{4,8},{8,12},{12,16},{16,20},{20,24},{24,28},{28,0},{1,5},{5... | collective-permute-start | bytes 3145736 | tf_op jit(solution)/shard_map/ppermute | solution.py:28
  312.8 253.8 %reduce-scatter.13.cloned.1.call-start = ((), (), s32[]{:S(2)}) async-start(), calls=%async_computation.18 | async-start | bytes 5242880 | tf_op jit(solution)/shard_map/reduce_scatter | solution.py:182
  312.8 27.0 %collective-permute-start.2 = (bf16[256,2048]{1,0:T(8,128)(2,1)}, bf16[256,2048]{1,0:T(8,128)(2,1)S(1)}, u32[]{:S(2)}, u32[]{:S(2)}) collective-permute-start(bf16[256,2048]{1,0:T(8,128)(2,1)} %collective-permute-done.1), channel_id=1, source_target_pairs={{0,4},{4,8},{8,12},{12,16},{16,20},{20,24},{24,28},{28,0},{1,5},{5... | collective-permute-start | bytes 3145736 | tf_op jit(solution)/shard_map/ppermute | solution.py:28
  340.8 32.6 %collective-permute-start.3 = (bf16[256,2048]{1,0:T(8,128)(2,1)S(1)}, bf16[256,2048]{1,0:T(8,128)(2,1)S(1)}, u32[]{:S(2)}, u32[]{:S(2)}) collective-permute-start(bf16[256,2048]{1,0:T(8,128)(2,1)S(1)} %collective-permute-done.2), channel_id=1, source_target_pairs={{0,4},{4,8},{8,12},{12,16},{16,20},{20,24},{24,28},{28,0},{1,5},{5... | collective-permute-start | bytes 3145736 | tf_op jit(solution)/shard_map/ppermute | solution.py:28
  374.4 15.4 %collective-permute-start.4 = (bf16[256,2048]{1,0:T(8,128)(2,1)S(1)}, bf16[256,2048]{1,0:T(8,128)(2,1)}, u32[]{:S(2)}, u32[]{:S(2)}) collective-permute-start(bf16[256,2048]{1,0:T(8,128)(2,1)S(1)} %collective-permute-done.3), channel_id=1, source_target_pairs={{0,4},{4,8},{8,12},{12,16},{16,20},{20,24},{24,28},{28,0},{1,5},{5... | collective-permute-start | bytes 3145736 | tf_op jit(solution)/shard_map/ppermute | solution.py:28
  389.8 15.4 %collective-permute-start.5 = (bf16[256,2048]{1,0:T(8,128)(2,1)}, bf16[256,2048]{1,0:T(8,128)(2,1)}, u32[]{:S(2)}, u32[]{:S(2)}) collective-permute-start(bf16[256,2048]{1,0:T(8,128)(2,1)} %collective-permute-done.4), channel_id=1, source_target_pairs={{0,4},{4,8},{8,12},{12,16},{16,20},{20,24},{24,28},{28,0},{1,5},{5... | collective-permute-start | bytes 3145736 | tf_op jit(solution)/shard_map/ppermute | solution.py:28
  405.2 15.3 %collective-permute-start.6 = (bf16[256,2048]{1,0:T(8,128)(2,1)}, bf16[256,2048]{1,0:T(8,128)(2,1)S(1)}, u32[]{:S(2)}, u32[]{:S(2)}) collective-permute-start(bf16[256,2048]{1,0:T(8,128)(2,1)} %collective-permute-done.5), channel_id=1, source_target_pairs={{0,4},{4,8},{8,12},{12,16},{16,20},{20,24},{24,28},{28,0},{1,5},{5... | collective-permute-start | bytes 3145736 | tf_op jit(solution)/shard_map/ppermute | solution.py:28
  490.1 161.9 %all-gather.24.cloned.1.call-start = ((), (), s32[]{:S(2)}) async-start(), calls=%async_computation.19 | async-start | bytes 5242880 | tf_op jit(solution)/shard_map/all_gather | solution.py:256
  570.7 185.2 %reduce-scatter.15.cloned.1.call-start = ((), (), s32[]{:S(2)}) async-start(), calls=%async_computation.20 | async-start | bytes 5242880 | tf_op jit(solution)/shard_map/reduce_scatter | solution.py:182
  680.5 166.7 %all-gather.26.cloned.1.call-start = ((), (), s32[]{:S(2)}) async-start(), calls=%async_computation.21 | async-start | bytes 5242880 | tf_op jit(solution)/shard_map/all_gather | solution.py:275
  765.7 237.2 %reduce-scatter.29.cloned.1.call-start = ((), (), s32[]{:S(2)}) async-start(), calls=%async_computation.28 | async-start | bytes 9437184 | tf_op jit(solution)/shard_map/reduce_scatter | solution.py:267
  780.3 225.5 %reduce-scatter.27.cloned.1.call-start = ((), (), s32[]{:S(2)}) async-start(), calls=%async_computation.27 | async-start | bytes 9437184 | tf_op jit(solution)/shard_map/reduce_scatter | solution.py:264
  794.4 245.3 %reduce-scatter.25.cloned.1.call-start = ((), (), s32[]{:S(2)}) async-start(), calls=%async_computation.26 | async-start | bytes 2359296 | tf_op jit(solution)/shard_map/reduce_scatter | solution.py:182
  853.2 230.9 %reduce-scatter.23.cloned.1.call-start = ((), (), s32[]{:S(2)}) async-start(), calls=%async_computation.25 | async-start | bytes 2359296 | tf_op jit(solution)/shard_map/reduce_scatter | solution.py:182
  975.1 153.3 %reduce-scatter.19.cloned.1.call-start = ((), (), s32[]{:S(2)}) async-start(), calls=%async_computation.23 | async-start | bytes 2359296 | tf_op jit(solution)/shard_map/reduce_scatter | solution.py:182
  982.6 190.0 %reduce-scatter.21.cloned.1.call-start = ((), (), s32[]{:S(2)}) async-start(), calls=%async_computation.24 | async-start | bytes 2359296 | tf_op jit(solution)/shard_map/reduce_scatter | solution.py:182
  988.9 262.9 %reduce-scatter.17.cloned.1.call-start = ((), (), s32[]{:S(2)}) async-start(), calls=%async_computation.22 | async-start | bytes 5242880 | tf_op jit(solution)/shard_map/reduce_scatter | solution.py:182
  1008.7 243.1 %copy-start.5 = (bf16[256,2048]{1,0:T(8,128)(2,1)S(1)}, bf16[256,2048]{1,0:T(8,128)(2,1)}, u32[]{:S(2)}) copy-start(bf16[256,2048]{1,0:T(8,128)(2,1)} %param.26) | copy-start | bytes 3145732
  1008.7 243.1 %copy-start.39 = (f32[2048]{0:T(1024)S(1)}, f32[2048]{0:T(1024)}, u32[]{:S(2)}) copy-start(f32[2048]{0:T(1024)} %param.27) | copy-start | bytes 24580
  1008.7 243.1 %copy-start.44 = (f32[256]{0:T(256)S(1)}, f32[256]{0:T(256)}, u32[]{:S(2)}) copy-start(f32[256]{0:T(256)} %copy-done.43) | copy-start | bytes 3076
  1041.6 212.1 %copy-start.52 = (f32[256]{0:T(256)S(1)}, f32[256]{0:T(256)}, u32[]{:S(2)}) copy-start(f32[256]{0:T(256)} %copy-done.51) | copy-start | bytes 3076
  1041.6 212.1 %copy-start.50 = (f32[256]{0:T(256)S(1)}, f32[256]{0:T(256)}, u32[]{:S(2)}) copy-start(f32[256]{0:T(256)} %copy-done.49) | copy-start | bytes 3076
  (73 other events, 1329.6 us)
Sparse Core Ops, SparseCore 0:
  9.9 30.5 all-gather.13
  42.7 80.7 all-gather.9
  125.4 26.2 all-gather.15
  153.4 27.7 all-gather.11
  183.0 27.7 all-gather.17
  231.9 76.7 reduce-scatter.10
  310.6 69.7 all-gather.21
  382.6 80.2 all-gather.19
  490.2 76.3 reduce-scatter.12
  570.8 81.1 all-gather.23
  680.6 75.2 reduce-scatter.14
  765.8 81.2 all-gather.25
  850.6 69.9 reduce-scatter.28
  923.9 71.4 reduce-scatter.26
  998.6 41.1 reduce-scatter.24
  1042.9 41.1 reduce-scatter.22
  1087.2 41.1 reduce-scatter.18
  1131.5 41.1 reduce-scatter.20
  1174.9 76.7 reduce-scatter.16
